TPU v7x, 256 devices: a whole 4x4x8 slice. The times are simulated.
256 devices in a mesh: row: 8 (over y, core), col: 32 (over x, z).
Axes of the slice: x: 4, y: 4, z: 8, core: 2. Of those that a mesh axis runs over, the one named last changes fastest.
Arguments:
- kkt: float32 [8192, 8192], P('row', 'col'), may hold values from -4 to 4, as said below
- swaps: int32 [2, 2, 128], replicated, may hold values from 0 to 8191, as said below
- inverses: float32 [2, 256, 256], replicated
- pivots: float32 [2, 256], replicated, may hold values from -0.12 to 0.12
- couplings: float32 [2, 256], replicated, may hold values from -0.12 to 0.12
- pattern: int32 [2, 256], replicated, may hold values from 0 to 1, as said below
Outputs:
- factored: float32 [8192, 8192], P('row', 'col')
Inputs may be any that keep to these rules, and one draw needn't show every extreme that they name: For panel k, swaps[k, 0, :] holds 128 distinct rows among k * 256 to k * 256 + 255, both ends of that range among them, and swaps[k, 1, :] holds 128 distinct rows among (k + 1) * 256 to 8191, both ends of that range among them. pattern[k, i] = 1 makes rows i and i + 1 one 2 x 2 block of D; no two neighbouring entries are both 1 and the last entry is 0. kkt is the stored order of a symmetric matrix.
All inputs are finite; a program needn't handle non-finite values.
Results may differ from a plain program's by a relative error of at most 0.00014.
Values sent between devices are 32-bit elements; how exact they have to be, the bound alone decides.
A program may use at most 64 MiB of HBM per device.

v0:
```python
import jax
import jax.numpy as jnp
from jax import lax
from jax.sharding import Mesh
from jax.sharding import PartitionSpec as P

COL = ("col_0", "col_1")
HI = lax.Precision.HIGHEST


def tdot(a, b):
    return lax.dot_general(
        a, b, (((0,), (0,)), ((), ())), precision=HI, preferred_element_type=jnp.float32
    )


def swapped(rows, lead, partner):
    to_partner = rows[:, None] == lead[None, :]
    to_lead = rows[:, None] == partner[None, :]
    moved = jnp.sum(
        jnp.where(to_partner, partner[None, :], 0) + jnp.where(to_lead, lead[None, :], 0), axis=1
    )
    return jnp.where(jnp.any(to_partner | to_lead, axis=1), moved, rows)


def plan(swaps, tile, row_groups, dtype=jnp.float32):
    width = tile // row_groups
    count = swaps.shape[2]
    partner = swaps[:, 1, :].reshape(-1)
    top = jnp.arange(2 * tile, dtype=jnp.int32)
    rows = jnp.concatenate([top, partner])
    source = swapped(swapped(rows, swaps[1, 0], swaps[1, 1]), swaps[0, 0], swaps[0, 1])
    repeated = jnp.any(swaps[0, 1][:, None] == swaps[1, 1][None, :], axis=1)
    valid = jnp.concatenate([~repeated, jnp.ones((count,), bool)]) & (partner >= 2 * tile)
    sliced = source.reshape(3, row_groups, width).transpose(1, 0, 2)
    return (rows, source, sliced, jnp.where(valid, partner, -1))


def hits(rows, first, tile):
    return (rows[:, None] == first + jnp.arange(tile, dtype=jnp.int32)[None, :]).astype(jnp.float32)


def along_d(lower_t, pivot, coupling, pattern):
    links = coupling * pattern.astype(jnp.float32)
    zero = jnp.zeros((1, lower_t.shape[1]), lower_t.dtype)
    after = jnp.concatenate([lower_t[1:], zero], axis=0)
    before = jnp.concatenate([zero, lower_t[:-1]], axis=0)
    links_before = jnp.concatenate([jnp.zeros((1,), links.dtype), links[:-1]])
    return lower_t * pivot[:, None] + after * links[:, None] + before * links_before[:, None]


def exchange(picked, moves, tile, row_groups, x_size):
    width = tile // row_groups
    row_index = lax.axis_index("row")
    z_index = lax.axis_index("col_1")
    piece = lax.psum_scatter(picked, "row", scatter_dimension=0, tiled=False)
    strip = lax.all_gather(piece, "row")
    mine = lax.psum(jnp.where(z_index == row_index, strip, 0.0), "col_1")
    wide = lax.all_gather(mine, "col_0")
    part = jnp.dot(piece, moves, precision=HI, preferred_element_type=jnp.float32)
    t0, t1, tp = (part[:width], part[width : 2 * width], part[2 * width :])
    corner = jnp.stack(
        [
            t0[:, 2 * tile :],
            t1[:, 2 * tile :],
            tp[:, 2 * tile :],
            t0[:, tile : 2 * tile],
            t0[:, :tile],
            t1[:, tile : 2 * tile],
        ]
    )
    corner = lax.all_gather(lax.psum(corner, COL), "row")
    return (strip, wide, corner)


def shards(kkt, swaps, inverses, pivots, couplings, pattern):
    tile = inverses.shape[1]
    row_groups = lax.axis_size("row")
    x_size = lax.axis_size("col_0")
    z_size = lax.axis_size("col_1")
    row_index = lax.axis_index("row")
    col_index = lax.axis_index(COL)
    rows, source, sliced, partner = plan(swaps, tile, row_groups)
    flat = sliced.reshape(-1)
    owned = flat // tile % row_groups == row_index
    taken = jnp.take(kkt, flat // tile // row_groups * tile + flat % tile, axis=0)
    picked = jnp.where(owned[:, None], taken, 0.0).reshape(row_groups, -1, tile)
    moves = hits(source, col_index * tile, tile).T
    strip, wide, corner = exchange(picked, moves, tile, row_groups, x_size)

    def ordered(piece):
        return piece.reshape(row_groups, 3, -1, tile).transpose(1, 0, 2, 3).reshape(-1, tile)

    corner = corner.transpose(1, 0, 2, 3).reshape(6, tile, tile)
    to_partner = corner[0:3].reshape(3 * tile, tile)
    block_01, block_00, block_11 = (corner[3], corner[4], corner[5])
    tiles = [row_index + row_groups * slot for slot in range(x_size)] + [col_index]
    strips = [ordered(wide[slot]) for slot in range(x_size)] + [ordered(strip)]
    marks = [hits(partner, index * tile, tile) for index in tiles]
    keep = [1.0 - jnp.sum(mark, axis=0) for mark in marks]
    fixed = [
        strips[n] * keep[n][None, :]
        + jnp.dot(to_partner, marks[n], precision=HI, preferred_element_type=jnp.float32)
        for n in range(x_size + 1)
    ]
    upper = [jnp.where(tiles[n] == 1, block_01, fixed[n][:tile]) for n in range(x_size + 1)]
    low0 = [jnp.where(tiles[n] > 0, tdot(inverses[0], upper[n]), 0.0) for n in range(x_size + 1)]
    low0_1 = tdot(inverses[0], block_01)
    scaled0_1 = along_d(low0_1, pivots[0], couplings[0], pattern[0])
    scaled0 = along_d(low0[-1], pivots[0], couplings[0], pattern[0])
    low1 = [
        jnp.where(
            tiles[n] > 1,
            tdot(inverses[1], fixed[n][tile : 2 * tile] - tdot(scaled0_1, low0[n])),
            0.0,
        )
        for n in range(x_size + 1)
    ]
    scaled1 = along_d(low1[-1], pivots[1], couplings[1], pattern[1])
    outs = []
    for n in range(x_size):
        base = kkt[n * tile : (n + 1) * tile] * keep[n][:, None] * keep[-1][None, :]
        base = base + tdot(marks[n], fixed[-1][2 * tile :])
        base = base + tdot(fixed[n][2 * tile :] * keep[n][None, :], marks[-1])
        value = base - tdot(low0[n], scaled0) - tdot(low1[n], scaled1)
        value = jnp.where(tiles[n] == 0, scaled0, value)
        value = jnp.where(tiles[n] == 1, scaled1, value)
        at_0 = jnp.where(tiles[n] == 0, block_00, low0[n].T)
        at_1 = jnp.where(tiles[n] == 0, scaled0_1, low1[n].T)
        at_1 = jnp.where(tiles[n] == 1, block_11 - tdot(low0_1, scaled0_1), at_1)
        value = jnp.where(col_index == 0, at_0, value)
        value = jnp.where(col_index == 1, at_1, value)
        outs.append(value)
    return jnp.concatenate(outs, axis=0)


def solution(mesh):
    z_size = mesh.shape["row"]
    finer = Mesh(mesh.devices.reshape(mesh.shape["row"], -1, z_size), ("row", "col_0", "col_1"))
    in_specs = (P("row", COL), P(), P(), P(), P(), P())
    return jax.shard_map(
        shards, mesh=finer, in_specs=in_specs, out_specs=P("row", COL), check_vma=False
    )
```

profile of v0, /device:TPU:1, one launch (start us, length us, event | category | flops | bytes accessed | tf_op | source)
XLA Modules:
  0.0 369.6 jit_solution(7685777161819229525)
XLA Ops:
  6.5 0.8 slice_bitcast_fusion.9
  7.3 0.7 slice.199
  9.6 3.3 gather_fusion
  12.9 1.2 select_select_fusion
  14.2 35.9 %reduce-scatter.2.cloned.1.call-done = f32[1,96,256]{2,1,0:T(8,128)} async-done(((f32[8,96,256]{2,1,0:T(8,128)}), f32[1,96,256]{2,1,0:T(8,128)}) %reduce-scatter.2.cloned.1.call-update) | async-done | bytes 98320 | tf_op jit(solution)/shard_map/reduce_scatter | solution.py:56
  50.1 1.5 fusion.17
  51.6 0.7 copy-done.4
  52.4 16.4 %all_gather.17 = f32[8,96,256]{2,1,0:T(8,128)S(1)} all-gather(f32[1,96,256]{2,1,0:T(8,128)} %reduce-scatter.2.cloned.1.call-done), channel_id=1, replica_groups=mesh['row'=8,'col_0'=4,'col_1'=8] {'row'}, dimensions={0}, use_global_device_ids=true | all-gather | bytes 884736 | tf_op jit(solution)/shard_map/all_gather | solution.py:57
  68.8 1.0 select_bitcast_fusion
  69.8 124.7 %all-reduce.10.cloned.1.call-done = f32[1,6,32,256]{3,2,1,0:T(8,128)} async-done(((f32[1,6,32,256]{3,2,1,0:T(8,128)}), f32[1,6,32,256]{3,2,1,0:T(8,128)}) %all-reduce.10.cloned.1.call-update) | async-done | bytes 196624 | tf_op jit(solution)/shard_map/psum | solution.py:72
  195.3 73.7 %all-reduce.12.cloned.1.call-done = f32[1,8,96,256]{3,2,1,0:T(8,128)} async-done(((f32[1,8,96,256]{3,2,1,0:T(8,128)}), f32[1,8,96,256]{3,2,1,0:T(8,128)}) %all-reduce.12.cloned.1.call-update) | async-done | bytes 786448 | tf_op jit(solution)/shard_map/psum | solution.py:58
  269.2 31.6 %all-gather.3.cloned.1.call-done = f32[8,6,32,256]{3,2,1,0:T(8,128)} async-done(((f32[1,6,32,256]{3,2,1,0:T(8,128)}), f32[8,6,32,256]{3,2,1,0:T(8,128)}) %all-gather.3.cloned.1.call-update) | async-done | bytes 1572880 | tf_op jit(solution)/shard_map/all_gather | solution.py:72
  300.8 1.5 copy.51
  302.4 0.8 fusion.125
  304.6 0.6 convolution_select_fusion.7
  305.5 0.6 convolution_subtract_fusion.11
  306.1 0.6 fusion.8
  307.3 1.2 convolution_add_fusion.6
  310.0 0.6 convolution_subtract_fusion.13
  310.6 33.6 %all-gather.5.cloned.1.call-done = f32[4,8,96,256]{3,2,1,0:T(8,128)} async-done(((f32[1,8,96,256]{3,2,1,0:T(8,128)}), f32[4,8,96,256]{3,2,1,0:T(8,128)}) %all-gather.5.cloned.1.call-update) | async-done | bytes 3145744 | tf_op jit(solution)/shard_map/all_gather | solution.py:59
  344.2 2.2 fusion.124
  350.0 0.6 convolution_select_fusion.1
  350.6 0.6 convolution_subtract_fusion.2
  351.7 0.6 convolution_select_fusion.3
  352.3 0.8 convolution_subtract_fusion.5
  354.3 0.6 convolution_select_fusion.5
  356.4 0.6 bitcast_select_fusion.3
  358.0 0.6 convolution_select_fusion
  358.6 0.6 convolution_select_fusion.2
  359.2 0.6 convolution_select_fusion.4
  359.8 0.6 convolution_select_fusion.8
  362.1 1.0 pad_maximum_fusion
  (99 shorter events, 15.6 us)
Async XLA Ops:
  6.5 43.5 %reduce-scatter.2.cloned.1.call-start = ((), (), s32[]{:S(2)}) async-start(), calls=%async_computation.1 | async-start | bytes 884736 | tf_op jit(solution)/shard_map/reduce_scatter | solution.py:56
  14.1 180.4 %all-reduce.10.cloned.1.call-start = ((), (), s32[]{:S(2)}) async-start(), calls=%async_computation.2 | async-start | bytes 393216 | tf_op jit(solution)/shard_map/psum | solution.py:72
  51.6 0.7 copy-start.4
  52.3 142.9 %copy-start.5 = (s32[2,256]{1,0:T(2,128)S(1)}, s32[2,256]{1,0:T(2,128)}, u32[]{:S(2)}) copy-start(s32[2,256]{1,0:T(2,128)} %param.11) | copy-start | bytes 6148
  52.3 142.9 %copy-start.6 = (f32[2,256]{1,0:T(2,128)S(1)}, f32[2,256]{1,0:T(2,128)}, u32[]{:S(2)}) copy-start(f32[2,256]{1,0:T(2,128)} %param.10) | copy-start | bytes 6148
  52.4 216.6 %all-reduce.12.cloned.1.call-start = ((), (), s32[]{:S(2)}) async-start(), calls=%async_computation.4 | async-start | bytes 1572864 | tf_op jit(solution)/shard_map/psum | solution.py:58
  68.8 200.2 %copy-start.7 = (f32[2,256]{1,0:T(2,128)S(1)}, f32[2,256]{1,0:T(2,128)}, u32[]{:S(2)}) copy-start(f32[2,256]{1,0:T(2,128)} %param.9) | copy-start | bytes 6148
  69.8 231.1 %all-gather.3.cloned.1.call-start = ((), (), s32[]{:S(2)}) async-start(), calls=%async_computation.3 | async-start | bytes 1769472 | tf_op jit(solution)/shard_map/all_gather | solution.py:72
  194.5 149.6 %all-gather.5.cloned.1.call-start = ((), (), s32[]{:S(2)}) async-start(), calls=%async_computation.5 | async-start | bytes 3932160 | tf_op jit(solution)/shard_map/all_gather | solution.py:59
  302.4 1.0 copy-start.1
  306.1 1.2 copy-start
  348.6 1.0 copy-start.2
  354.9 1.5 copy-start.3
Sparse Core Ops, SparseCore 0:
  14.2 35.8 reduce-scatter.1
  53.5 140.9 all-reduce.9
  196.8 72.0 all-reduce.11
  270.6 30.1 all-gather.2
  302.5 41.6 all-gather.4
where the time goes:
time: 370 us
  waiting for transfers between devices  300 us (81%)
  matrix products  22.2 us (6%)
  blocking collectives  16.4 us (4%)
  between operations  13.9 us (4%)
  local copies, waits for them, and re-layouts  11.6 us (3%)
  other arithmetic  5.64 us (2%)
    psum x1, waiting for transfers between devices, exchange(): corner = lax.all_gather(lax.psum(corner, COL), 'row')  125 us
    psum x1, waiting for transfers between devices, exchange(): mine = lax.psum(jnp.where(z_index == row_index, strip, 0.0), 'col_1')  73.7 us
    reduce_scatter x1, waiting for transfers between devices, exchange(): piece = lax.psum_scatter(picked, 'row', scatter_dimension=0, tiled=False)  35.9 us
    all_gather x1, waiting for transfers between devices, exchange(): wide = lax.all_gather(mine, 'col_0')  33.6 us
    all_gather x1, waiting for transfers between devices, exchange(): corner = lax.all_gather(lax.psum(corner, COL), 'row')  31.6 us
    dot_general x33, matrix products, tdot(): lax.dot_general(a, b, (((0,), (0,)), ((), ())), precision=HI, preferred_e...  17.9 us
    all_gather x1, blocking collectives, exchange(): strip = lax.all_gather(piece, 'row')  16.4 us
  transfers between devices with their start and end apart: 5, of which 5 were waited for; matrix products, arithmetic and copies ran while one was open for 3% of the time, Pallas kernels for 0%

commit v1 on v0

--- a/solution.py
+++ b/solution.py
@@ -55,7 +55,7 @@
     z_index = lax.axis_index("col_1")
     piece = lax.psum_scatter(picked, "row", scatter_dimension=0, tiled=False)
     strip = lax.all_gather(piece, "row")
-    mine = lax.psum(jnp.where(z_index == row_index, strip, 0.0), "col_1")
+    mine = jnp.sum(lax.all_gather(jnp.where(z_index == row_index, strip, 0.0), "col_1"), axis=0)
     wide = lax.all_gather(mine, "col_0")
     part = jnp.dot(piece, moves, precision=HI, preferred_element_type=jnp.float32)
     t0, t1, tp = (part[:width], part[width : 2 * width], part[2 * width :])

time: 370 us -> 369 us (level)
  waiting for transfers between devices: 300 us -> 295 us
  other arithmetic: 5.64 us -> 9.82 us
    all_gather x0 -> x1, waiting for transfers between devices: none -> 77.2 us  [exchange(): lax.all_gather(jnp.where(z_index == row_index, strip, 0.0), 'col_1')]
    psum x1 -> x0, waiting for transfers between devices: 73.7 us -> none  [exchange(): mine = lax.psum(jnp.where(z_index == row_index, strip, 0.0), 'col_1')]
    all_gather x1, waiting for transfers between devices: 31.6 us -> 23.3 us  [exchange(): corner = lax.all_gather(lax.psum(corner, COL), 'row')]
    reduce_sum x0 -> x1, other arithmetic: none -> 4.18 us  [exchange(): jnp.sum(lax.all_gather(jnp.where(z_index == row_index, strip, 0.0), 'col_...]
  transfers between devices with their start and end apart: 5 -> 5, of which waited for: 5 -> 5; matrix products, arithmetic and copies ran while one was open for 3% -> 4% of each run, Pallas kernels for 0% -> 0%
where the time goes in v1:
time: 369 us
  waiting for transfers between devices  295 us (80%)
  matrix products  22.2 us (6%)
  blocking collectives  16.4 us (4%)
  between operations  13.9 us (4%)
  local copies, waits for them, and re-layouts  10.7 us (3%)
  other arithmetic  9.82 us (3%)
    psum x1, waiting for transfers between devices, exchange(): corner = lax.all_gather(lax.psum(corner, COL), 'row')  125 us
    all_gather x1, waiting for transfers between devices, exchange(): lax.all_gather(jnp.where(z_index == row_index, strip, 0.0), 'col_1')  77.2 us
    reduce_scatter x1, waiting for transfers between devices, exchange(): piece = lax.psum_scatter(picked, 'row', scatter_dimension=0, tiled=False)  35.9 us
    all_gather x1, waiting for transfers between devices, exchange(): wide = lax.all_gather(mine, 'col_0')  34.2 us
    all_gather x1, waiting for transfers between devices, exchange(): corner = lax.all_gather(lax.psum(corner, COL), 'row')  23.3 us
    dot_general x33, matrix products, tdot(): lax.dot_general(a, b, (((0,), (0,)), ((), ())), precision=HI, preferred_e...  17.9 us
    all_gather x1, blocking collectives, exchange(): strip = lax.all_gather(piece, 'row')  16.4 us
  transfers between devices with their start and end apart: 5, of which 5 were waited for; matrix products, arithmetic and copies ran while one was open for 4% of the time, Pallas kernels for 0%

profile of v1, /device:TPU:1, one launch (start us, length us, event | category | flops | bytes accessed | tf_op | source)
XLA Modules:
  0.0 368.7 jit_solution(3839044218326096964)
XLA Ops:
  6.5 0.7 slice.199
  7.2 0.8 slice_bitcast_fusion.9
  9.6 3.3 gather_fusion
  12.9 1.2 select_select_fusion
  14.2 35.9 %reduce-scatter.2.cloned.1.call-done = f32[1,96,256]{2,1,0:T(8,128)} async-done(((f32[8,96,256]{2,1,0:T(8,128)}), f32[1,96,256]{2,1,0:T(8,128)}) %reduce-scatter.2.cloned.1.call-update) | async-done | bytes 98320 | tf_op jit(solution)/shard_map/reduce_scatter | solution.py:56
  50.1 1.5 fusion.17
  51.7 0.7 copy-done.4
  52.4 16.4 %all_gather.23 = f32[8,96,256]{2,1,0:T(8,128)S(1)} all-gather(f32[1,96,256]{2,1,0:T(8,128)} %reduce-scatter.2.cloned.1.call-done), channel_id=1, replica_groups=mesh['row'=8,'col_0'=4,'col_1'=8] {'row'}, dimensions={0}, use_global_device_ids=true | all-gather | bytes 884736 | tf_op jit(solution)/shard_map/all_gather | solution.py:57
  68.8 1.0 broadcast_select_fusion
  69.8 124.7 %all-reduce.9.cloned.1.call-done = f32[1,6,32,256]{3,2,1,0:T(8,128)} async-done(((f32[1,6,32,256]{3,2,1,0:T(8,128)}), f32[1,6,32,256]{3,2,1,0:T(8,128)}) %all-reduce.9.cloned.1.call-update) | async-done | bytes 196624 | tf_op jit(solution)/shard_map/psum | solution.py:72
  195.3 77.2 %all-gather.8.cloned.1.call-done = f32[64,96,256]{2,1,0:T(8,128)} async-done(((f32[8,96,256]{2,1,0:T(8,128)}), f32[64,96,256]{2,1,0:T(8,128)}) %all-gather.8.cloned.1.call-update) | async-done | bytes 6291472 | tf_op jit(solution)/shard_map/all_gather | solution.py:58
  272.5 4.2 %reduce_sum.74 = f32[8,96,256]{2,1,0:T(8,128)} reduce(f32[8,8,96,256]{3,2,1,0:T(8,128)} %bitcast.169, f32[]{:T(128)} %constant.92.clone.1), dimensions={0}, to_apply=%region_6.7 | reduce | flops 1376256 | bytes 7077892 | tf_op jit(solution)/shard_map/reduce_sum | solution.py:58
  277.0 23.3 %all-gather.6.cloned.1.call-done = f32[8,6,32,256]{3,2,1,0:T(8,128)} async-done(((f32[1,6,32,256]{3,2,1,0:T(8,128)}), f32[8,6,32,256]{3,2,1,0:T(8,128)}) %all-gather.6.cloned.1.call-update) | async-done | bytes 1572880 | tf_op jit(solution)/shard_map/all_gather | solution.py:72
  300.3 1.5 copy.52
  301.9 0.8 fusion.125
  302.7 0.6 fusion.55
  303.8 0.6 convolution_select_fusion.7
  304.7 0.6 convolution_subtract_fusion.11
  305.3 0.6 fusion.8
  307.6 1.2 convolution_add_fusion.6
  308.8 0.6 convolution_subtract_fusion.13
  309.4 34.2 %all-gather.10.cloned.1.call-done = f32[32,96,256]{2,1,0:T(8,128)} async-done(((f32[8,96,256]{2,1,0:T(8,128)}), f32[32,96,256]{2,1,0:T(8,128)}) %all-gather.10.cloned.1.call-update) | async-done | bytes 3145744 | tf_op jit(solution)/shard_map/all_gather | solution.py:59
  343.6 2.2 fusion.124
  349.1 0.6 convolution_select_fusion.1
  350.7 0.8 convolution_select_fusion.3
  352.6 0.6 convolution_select_fusion.5
  354.3 0.6 bitcast_select_fusion.3
  357.1 0.6 convolution_select_fusion.8
  357.7 0.6 convolution_select_fusion.4
  358.3 0.6 convolution_select_fusion.2
  358.9 0.6 convolution_select_fusion
  361.1 1.0 pad_maximum_fusion
  (100 shorter events, 15.2 us)
Async XLA Ops:
  6.5 43.6 %reduce-scatter.2.cloned.1.call-start = ((), (), s32[]{:S(2)}) async-start(), calls=%async_computation.1 | async-start | bytes 884736 | tf_op jit(solution)/shard_map/reduce_scatter | solution.py:56
  12.9 182.3 %copy-start.5 = (s32[2,256]{1,0:T(2,128)S(1)}, s32[2,256]{1,0:T(2,128)}, u32[]{:S(2)}) copy-start(s32[2,256]{1,0:T(2,128)} %param.11) | copy-start | bytes 6148
  12.9 182.3 %copy-start.6 = (f32[2,256]{1,0:T(2,128)S(1)}, f32[2,256]{1,0:T(2,128)}, u32[]{:S(2)}) copy-start(f32[2,256]{1,0:T(2,128)} %param.10) | copy-start | bytes 6148
  14.1 180.4 %all-reduce.9.cloned.1.call-start = ((), (), s32[]{:S(2)}) async-start(), calls=%async_computation.2 | async-start | bytes 393216 | tf_op jit(solution)/shard_map/psum | solution.py:72
  51.7 0.7 copy-start.4
  52.4 220.2 %all-gather.8.cloned.1.call-start = ((), (), s32[]{:S(2)}) async-start(), calls=%async_computation.4 | async-start | bytes 7077888 | tf_op jit(solution)/shard_map/all_gather | solution.py:58
  69.8 230.5 %all-gather.6.cloned.1.call-start = ((), (), s32[]{:S(2)}) async-start(), calls=%async_computation.3 | async-start | bytes 1769472 | tf_op jit(solution)/shard_map/all_gather | solution.py:72
  194.5 149.1 %all-gather.10.cloned.1.call-start = ((), (), s32[]{:S(2)}) async-start(), calls=%async_computation.5 | async-start | bytes 3932160 | tf_op jit(solution)/shard_map/all_gather | solution.py:59
  272.5 4.3 %copy-start.7 = (f32[2,256]{1,0:T(2,128)S(1)}, f32[2,256]{1,0:T(2,128)}, u32[]{:S(2)}) copy-start(f32[2,256]{1,0:T(2,128)} %param.9) | copy-start | bytes 6148
  277.0 25.7 %copy-start.1 = (f32[2,256,256]{2,1,0:T(8,128)S(1)}, f32[2,256,256]{2,1,0:T(8,128)}, u32[]{:S(2)}) copy-start(f32[2,256,256]{2,1,0:T(8,128)} %param.8) | copy-start | bytes 1572868
  304.5 1.6 copy-start
  346.9 1.7 copy-start.2
  350.3 4.0 %copy-start.3 = (f32[1,8,32,256]{3,2,1,0:T(8,128)S(1)}, f32[1,8,32,256]{3,2,1,0:T(8,128)}, u32[]{:S(2)}) copy-start(f32[1,8,32,256]{3,2,1,0:T(8,128)} %get-tuple-element.15) | copy-start | bytes 786436
Sparse Core Ops, SparseCore 0:
  14.2 35.8 reduce-scatter.1
  53.5 140.9 all-reduce.8
  196.3 76.1 all-gather.7
  274.2 26.0 all-gather.5
  301.9 41.6 all-gather.9
